TPU v7x, 32 devices: a whole 2x2x4 slice. The times are simulated.
32 devices in a mesh: enc: 4 (over z), ctx: 8 (over y, x, core).
Axes of the slice: x: 2, y: 2, z: 4, core: 2. Of those that a mesh axis runs over, the one named last changes fastest.
Arguments:
- patches: bfloat16 [3072, 1280], P('enc'), may hold values from -17 to 17
- patch_image: int32 [3072], P('enc'), may hold values from 63 to 767, as said below
- vit_gain: float32 [1280], replicated, may hold values from 0.1 to 1.9
- vit_qkv: bfloat16 [1280, 16, 240], P(None, 'ctx')
- vit_proj: bfloat16 [1280, 1280], P('ctx'), may hold values from -0.15625 to 0.15625
- merge_gain: float32 [1280], replicated, may hold values from 0.1 to 1.9
- merge_up: bfloat16 [5120, 5120], P(None, 'ctx'), may hold values from -0.078125 to 0.078125
- merge_down: bfloat16 [5120, 8192], P('ctx', 'enc'), may hold values from -0.078125 to 0.078125
- text_embed: bfloat16 [3072, 8192], P('ctx', 'enc'), may hold values from -17 to 17
- placeholder_unit: int32 [3072], replicated, may hold values from -1 to 767, as said below
- doc_id: int32 [3072], replicated, may hold values from 0 to 15, never falling along the last dimension, each value on 1 to 1920 neighbouring positions
- dec_gain: float32 [8192], replicated, may hold values from 0.1 to 1.9
- dec_wq: bfloat16 [8192, 2048], P(None, 'enc')
- dec_wk: bfloat16 [8192, 512], P(None, 'enc')
- dec_wv: bfloat16 [8192, 512], P(None, 'enc'), may hold values from -0.0625 to 0.0625
Outputs:
- attended: bfloat16 [3072, 2048], P('ctx', 'enc')
Inputs may be any that keep to these rules, and one draw needn't show every extreme that they name: `patch_image`: the patches of an image are consecutive, start at a multiple of 4, number a multiple of 4 and at most 256, and lie within one aligned block of 768 patches; image numbers never fall and differ between images; in every such block some image has exactly 256 patches. `placeholder_unit`: -1 marks a text position. Every unit appears exactly once; the units of one image fill consecutive placeholders in their order; the placeholders of an aligned block of 384 positions are consecutive and number at most 192, and some block holds exactly 192. `doc_id`: document numbers never fall; a document has at most 1920 positions, and some document exactly 1920.
All inputs are finite; a program needn't handle non-finite values.
Results may differ from a plain program's by a relative error of at most 0.0085.
Values may be sent and summed in bfloat16 or wider, within the bound.
No kernel may reach another device: no remote copies, remote signals or barrier semaphores. Data moves between devices by JAX's collectives and lax.ppermute only.
A program may use at most 128 MiB of HBM per device.

v0:
```python
import math
import jax
import jax.numpy as jnp
from jax import lax
from jax.sharding import PartitionSpec as P

HD = 128
QPK = 4
EPSILON = 1e-06
NEGATIVE = -1e30


def layer_norm(values, scaling):
    widened = values.astype(jnp.float32)
    center = widened - jnp.mean(widened, axis=1, keepdims=True)
    spread = jnp.mean(center * center, axis=1, keepdims=True)
    return (center * lax.rsqrt(spread + EPSILON) * scaling).astype(jnp.bfloat16)


def image_attention(queries, keys_in, values_in, image_ids):
    head_count, row_count, head_width = queries.shape
    block_rows = math.gcd(row_count, 512)
    scaling = head_width ** (-0.5)

    def image_one_block(offset):
        query_block = lax.dynamic_slice_in_dim(queries, offset, block_rows, 1)
        block_ids = lax.dynamic_slice_in_dim(image_ids, offset, block_rows, 0)
        allowed = block_ids[:, None] == image_ids[None, :]
        scores = (
            jnp.einsum("hqd,hkd->hqk", query_block, keys_in, preferred_element_type=jnp.float32)
            * scaling
        )
        scores = jnp.where(allowed[None], scores, NEGATIVE)
        highest = jnp.max(scores, axis=2, keepdims=True)
        weights = jnp.exp(scores - highest)
        totals = jnp.sum(weights, axis=2, keepdims=True)
        mixture = jnp.einsum(
            "hqk,hkd->hqd",
            weights.astype(jnp.bfloat16),
            values_in,
            preferred_element_type=jnp.float32,
        )
        return (mixture / totals).astype(jnp.bfloat16)

    offsets = jnp.arange(row_count // block_rows, dtype=jnp.int32) * block_rows
    blocks = lax.map(image_one_block, offsets)
    return blocks.transpose(1, 0, 2, 3).reshape(head_count, row_count, head_width)


def body(
    patches,
    patch_image,
    vit_gain,
    vit_qkv,
    vit_proj,
    merge_gain,
    merge_up,
    merge_down,
    text_embed,
    placeholder_unit,
    doc_id,
    dec_gain,
    dec_wq,
    dec_wk,
    dec_wv,
):
    ctx_index = lax.axis_index("ctx")
    group_rows = patches.shape[0]
    head_count = vit_qkv.shape[1]
    head_width = vit_qkv.shape[2] // 3
    normed_patches = layer_norm(patches, vit_gain)
    packed = jnp.dot(
        normed_patches,
        vit_qkv.reshape(vit_qkv.shape[0], head_count * 3 * head_width),
        preferred_element_type=jnp.float32,
    )
    packed = (
        packed.astype(jnp.bfloat16)
        .reshape(group_rows, head_count, 3, head_width)
        .transpose(2, 1, 0, 3)
    )
    attended_patches = image_attention(packed[0], packed[1], packed[2], patch_image)
    flat_heads = attended_patches.transpose(1, 0, 2).reshape(group_rows, head_count * head_width)
    head_terms = jnp.dot(flat_heads, vit_proj, preferred_element_type=jnp.float32)
    summed = lax.psum(head_terms, "ctx")
    vit_out = (patches.astype(jnp.float32) + summed).astype(jnp.bfloat16)
    merge_input = layer_norm(lax.optimization_barrier(vit_out), merge_gain)
    unit_inputs = merge_input.reshape(group_rows // 4, 4 * merge_input.shape[1])
    hidden = jax.nn.gelu(
        jnp.dot(unit_inputs, merge_up, preferred_element_type=jnp.float32), approximate=False
    ).astype(jnp.bfloat16)
    all_hidden = lax.all_gather(hidden, "enc", axis=0, tiled=True)
    unit_total = all_hidden.shape[0]
    tok_rows = text_embed.shape[0]
    local_units = lax.dynamic_slice_in_dim(placeholder_unit, ctx_index * tok_rows, tok_rows, 0)
    present = local_units >= 0
    own_vision = lax.psum_scatter(
        jnp.dot(all_hidden, merge_down, preferred_element_type=jnp.float32),
        "ctx",
        scatter_dimension=0,
        tiled=True,
    ).astype(jnp.bfloat16)
    vision_all = lax.all_gather(own_vision, "ctx", axis=0, tiled=True)
    vision_local = jnp.take(vision_all, jnp.clip(local_units, 0, unit_total - 1), axis=0)
    sequence = jnp.where(present[:, None], vision_local, text_embed)
    full_rows = lax.all_gather(sequence, "enc", axis=1, tiled=True)
    widened = full_rows.astype(jnp.float32)
    row_scale = lax.rsqrt(jnp.mean(widened * widened, axis=1, keepdims=True) + EPSILON)
    normed = (widened * row_scale * dec_gain).astype(jnp.bfloat16)
    queries_flat = jnp.dot(normed, dec_wq, preferred_element_type=jnp.float32).astype(jnp.bfloat16)
    keys_local = jnp.dot(normed, dec_wk, preferred_element_type=jnp.float32).astype(jnp.bfloat16)
    values_local = jnp.dot(normed, dec_wv, preferred_element_type=jnp.float32).astype(jnp.bfloat16)
    kv_local = dec_wk.shape[1] // HD
    queries = queries_flat.reshape(tok_rows, kv_local, QPK, HD).transpose(1, 2, 0, 3)
    query_first = ctx_index * tok_rows
    query_pos = query_first + jnp.arange(tok_rows, dtype=jnp.int32)
    query_docs = lax.dynamic_slice_in_dim(doc_id, query_first, tok_rows, 0)
    scaling = HD ** (-0.5)
    start_state = (
        jnp.full((kv_local, QPK, tok_rows), NEGATIVE, jnp.float32),
        jnp.zeros((kv_local, QPK, tok_rows), jnp.float32),
        jnp.zeros((kv_local, QPK, tok_rows, HD), jnp.float32),
    )
    offset = jnp.int32(0)
    key_part = lax.all_gather(keys_local, "ctx", axis=0, tiled=True)
    value_part = lax.all_gather(values_local, "ctx", axis=0, tiled=True)
    key_count = key_part.shape[0]
    sub_rows = math.gcd(key_count, 512)
    last_doc = lax.dynamic_slice_in_dim(doc_id, offset + key_count - 1, 1, 0)[0]
    visible = (offset <= query_first + tok_rows - 1) & (last_doc >= query_docs[0])

    def update(current):

        def update_one_block(turn_index, inner_state):
            highest, totals, mixture = inner_state
            begin_row = turn_index * sub_rows
            keys_block = lax.dynamic_slice_in_dim(key_part, begin_row, sub_rows, 0).reshape(
                sub_rows, kv_local, HD
            )
            values_block = lax.dynamic_slice_in_dim(value_part, begin_row, sub_rows, 0).reshape(
                sub_rows, kv_local, HD
            )
            key_pos = begin_row + jnp.arange(sub_rows, dtype=jnp.int32)
            key_docs = lax.dynamic_slice_in_dim(doc_id, begin_row, sub_rows, 0)
            allowed = (key_pos[None, :] <= query_pos[:, None]) & (
                key_docs[None, :] == query_docs[:, None]
            )
            scores = (
                jnp.einsum(
                    "gjtd,sgd->gjts", queries, keys_block, preferred_element_type=jnp.float32
                )
                * scaling
            )
            new_peak = jnp.maximum(highest, jnp.max(jnp.where(allowed, scores, NEGATIVE), axis=3))
            factor = jnp.exp(highest - new_peak)
            weights = jnp.where(allowed, jnp.exp(scores - new_peak[..., None]), 0.0)
            totals = totals * factor + jnp.sum(weights, axis=3)
            mixture = mixture * factor[..., None] + jnp.einsum(
                "gjts,sgd->gjtd",
                weights.astype(jnp.bfloat16),
                values_block,
                preferred_element_type=jnp.float32,
            )
            return (new_peak, totals, mixture)

        return lax.fori_loop(0, key_count // sub_rows, update_one_block, current)

    def unchanged(current):
        return current

    finished = lax.cond(visible, update, unchanged, start_state)
    outputs = (finished[2] / finished[1][..., None]).astype(jnp.bfloat16)
    return outputs.transpose(2, 0, 1, 3).reshape(tok_rows, kv_local * QPK * HD)


def solution(mesh):
    placed = (
        P("enc", None),
        P("enc"),
        P(),
        P(None, "ctx", None),
        P("ctx", None),
        P(),
        P(None, "ctx"),
        P("ctx", "enc"),
        P("ctx", "enc"),
        P(),
        P(),
        P(),
        P(None, "enc"),
        P(None, "enc"),
        P(None, "enc"),
    )
    return jax.shard_map(
        body, mesh=mesh, in_specs=placed, out_specs=P("ctx", "enc"), check_vma=False
    )
```

profile of v0, /device:TPU:0, one launch (start us, length us, event | category | flops | bytes accessed | tf_op | source)
XLA Modules:
  0.0 467.7 jit_solution(1278942646428029388)
XLA Ops:
  11.7 14.6 %while.28 = (s32[]{:T(128)}, bf16[3,2,256,80]{2,3,1,0:T(8,128)(2,1)}, s32[3]{0:T(128)S(1)}, s32[768]{0:T(1024)S(1)}, bf16[2,768,80]{1,2,0:T(8,128)(2,1)S(1)}, /*...) while((s32[]{:T(128)}, ...), condition=%wide.region_5.6_spmd, body=%wide.region_2.5_spmd.sunk | while | flops 128859136 | bytes 6767287 | solution.py:46
  29.9 80.8 %all-reduce.2.cloned.1.call-done = f32[768,1280]{1,0:T(8,128)} async-done(((f32[768,1280]{1,0:T(8,128)}), f32[768,1280]{1,0:T(8,128)}) %all-reduce.2.cloned.1.call-update) | async-done | bytes 3932176 | tf_op jit(solution)/shard_map/psum | solution.py:85
  110.6 3.1 fusion.50
  116.8 4.1 reshape.149
  120.8 6.1 %fusion.61 = bf16[192,640]{1,0:T(8,128)(2,1)S(1)} fusion(bf16[192,5120]{1,0:T(8,128)(2,1)} %reshape.149, bf16[5120,640]{1,0:T(8,128)(2,1)} %param.27), kind=kOutput, calls=%fused_computation.81 | convolution fusion | flops 1266278400 | bytes 8765440 | tf_op jit(solution)/shard_map/dot_general | solution.py:90
  127.0 21.8 %all_gather.15 = bf16[768,640]{1,0:T(8,128)(2,1)S(1)} all-gather(bf16[192,640]{1,0:T(8,128)(2,1)S(1)} %fusion.61), channel_id=1, replica_groups=mesh['enc'=4,'ctx'=8] {'enc'}, dimensions={0}, use_global_device_ids=true | all-gather | bytes 1228800 | tf_op jit(solution)/shard_map/all_gather | solution.py:92
  148.8 4.5 fusion.75
  153.3 60.7 %reduce-scatter.2.cloned.1.call-done = f32[96,2048]{1,0:T(8,128)} async-done(((f32[768,2048]{1,0:T(8,128)}), f32[96,2048]{1,0:T(8,128)}) %reduce-scatter.2.cloned.1.call-update) | async-done | bytes 786448 | tf_op jit(solution)/shard_map/reduce_scatter | solution.py:97
  217.0 31.3 %all-gather.3.cloned.1.call-done = bf16[768,2048]{1,0:T(8,128)(2,1)} async-done(((bf16[96,2048]{1,0:T(8,128)(2,1)}), bf16[768,2048]{1,0:T(8,128)(2,1)}) %all-gather.3.cloned.1.call-update) | async-done | bytes 3145744 | tf_op jit(solution)/shard_map/all_gather | solution.py:103
  248.3 6.7 %gather_fusion = bf16[384,2048]{1,0:T(8,128)(2,1)S(1)} fusion(bf16[768,2048]{1,0:T(8,128)(2,1)} %all-gather.3.cloned.1.call-done, s32[1024]{0:T(1024)S(1)} %pad_clamp_fusion), kind=kCustom, calls=%fused_computation | custom fusion | bytes 3147264 | tf_op jit(solution)/shard_map/jit(_take)/gather | solution.py:104
  260.3 111.6 %all-gather.5.cloned.1.call-done = bf16[384,8192]{1,0:T(8,128)(2,1)} async-done(((bf16[384,2048]{1,0:T(8,128)(2,1)}), bf16[384,8192]{1,0:T(8,128)(2,1)}) %all-gather.5.cloned.1.call-update) | async-done | bytes 6291472 | tf_op jit(solution)/shard_map/all_gather | solution.py:106
  371.9 4.3 fusion.37
  376.5 3.7 convolution_convert_fusion.1
  380.2 11.4 %all_gather.19 = bf16[3072,128]{1,0:T(8,128)(2,1)} all-gather(bf16[384,128]{1,0:T(8,128)(2,1)S(1)} %convolution_convert_fusion.1), channel_id=1, replica_groups=mesh['enc'=4,'ctx'=8] {'ctx'}, dimensions={0}, use_global_device_ids=true | all-gather | bytes 884736 | tf_op jit(solution)/shard_map/all_gather | solution.py:126
  391.6 3.4 convolution_convert_fusion
  396.0 4.6 convolution_convert_fusion.2
  400.6 11.5 %all_gather.18 = bf16[3072,128]{1,0:T(8,128)(2,1)} all-gather(bf16[384,128]{1,0:T(8,128)(2,1)S(1)} %convolution_convert_fusion.2), channel_id=1, replica_groups=mesh['enc'=4,'ctx'=8] {'ctx'}, dimensions={0}, use_global_device_ids=true | all-gather | bytes 884736 | tf_op jit(solution)/shard_map/all_gather | solution.py:125
  412.2 46.3 %conditional.1 = (f32[1,4,384]{2,1,0:T(4,128)}, f32[1,4,384,128]{3,2,1,0:T(8,128)}) conditional(s32[]{:T(128)} %convert_element_type.60, () %tuple.31, (s32[]{:T(128)}, s32[384]{0:T(512)S(1)}, s32[3072]{0:T(1024)}, s32[384]{0:T(512)S(1)}, bf16[3072,128]{1,0:T(8,128)(2,1)}, /*index=5*/bf16[1,4,384,128]{3,2,1,0:T(8,128)(2,1)}, ...), branch_computations={%region_11.12_spmd, %region_12.17_spmd} | conditional | flops 412493696 | bytes 12566875 | solution.py:171
  412.2 46.3 %while.27 = (s32[]{:T(128)}, f32[1,4,384]{2,1,0:T(4,128)S(1)}, f32[1,4,384]{2,1,0:T(4,128)}, f32[1,4,384,128]{3,2,1,0:T(8,128)}, s32[384]{0:T(512)S(1)}, /*index...) while((s32[]{:T(128)}, f32[1,4,384]{2,1,0:T(4,128)S(1)}, ...), condition=%wide.region_16.16_spmd.clone, body=%wide.region_13.15_spmd.clone.sunk | while | flops 412493312 | bytes 12563663 | solution.py:166
  421.8 3.1 fusion.111
  429.7 3.1 fusion.111
  437.6 3.1 fusion.111
  445.5 3.1 fusion.111
  453.4 3.1 fusion.111
  (144 shorter events, 62.7 us)
Async XLA Ops:
  6.5 142.2 %copy-start = (bf16[640,2048]{1,0:T(8,128)(2,1)S(1)}, bf16[640,2048]{1,0:T(8,128)(2,1)}, u32[]{:S(2)}) copy-start(bf16[640,2048]{1,0:T(8,128)(2,1)} %param.28) | copy-start | bytes 7864324
  6.5 3.0 copy-start.12
  6.5 104.1 %all-reduce.2.cloned.1.call-start = ((), (), s32[]{:S(2)}) async-start(), calls=%async_computation.1 | async-start | bytes 7864320 | tf_op jit(solution)/shard_map/psum | solution.py:85
  6.5 2.3 copy-start.2
  6.6 3.0 copy-start.10
  9.5 2.1 copy-start.7
  11.7 15.5 %copy-start.5 = (bf16[160,1280]{1,0:T(8,128)(2,1)S(1)}, bf16[160,1280]{1,0:T(8,128)(2,1)}, u32[]{:S(2)}) copy-start(bf16[160,1280]{1,0:T(8,128)(2,1)} %param.25) | copy-start | bytes 1228804
  13.9 1.4 copy-start.6
  18.8 1.4 copy-start.6
  23.6 1.4 copy-start.6
  29.8 184.1 %reduce-scatter.2.cloned.1.call-start = ((), (), s32[]{:S(2)}) async-start(), calls=%async_computation.2 | async-start | bytes 7077888 | tf_op jit(solution)/shard_map/reduce_scatter | solution.py:97
  113.8 1.0 copy-start.8
  153.2 95.0 %all-gather.3.cloned.1.call-start = ((), (), s32[]{:S(2)}) async-start(), calls=%async_computation.3 | async-start | bytes 3538944 | tf_op jit(solution)/shard_map/all_gather | solution.py:103
  215.9 156.0 %all-gather.5.cloned.1.call-start = ((), (), s32[]{:S(2)}) async-start(), calls=%async_computation.4 | async-start | bytes 7864320 | tf_op jit(solution)/shard_map/all_gather | solution.py:106
  217.0 38.0 %copy-start.4 = (bf16[384,2048]{1,0:T(8,128)(2,1)S(1)}, bf16[384,2048]{1,0:T(8,128)(2,1)}, u32[]{:S(2)}) copy-start(bf16[384,2048]{1,0:T(8,128)(2,1)} %param.29) | copy-start | bytes 4718596
  256.4 119.8 %copy-start.11 = (f32[8192]{0:T(1024)S(1)}, f32[8192]{0:T(1024)}, u32[]{:S(2)}) copy-start(f32[8192]{0:T(1024)} %param.32) | copy-start | bytes 98308
  371.9 4.6 copy-start.3
  371.9 19.7 %slice-start = ((s8[8388608]{0:T(1024)(128)(4,1)}), s8[4194304]{0:T(1024)(128)(4,1)S(1)}, s32[]{:S(2)}) async-start(s8[8388608]{0:T(1024)(128)(4,1)} %bitcast.126), calls=%async_computation.5 | async-start | bytes 8388608
  376.5 15.1 %slice-start.1 = ((s8[8388608]{0:T(1024)(128)(4,1)}), s8[4194304]{0:T(1024)(128)(4,1)S(1)}, s32[]{:S(2)}) async-start(s8[8388608]{0:T(1024)(128)(4,1)} %bitcast.126), calls=%async_computation.6 | async-start | bytes 8388608
  391.6 4.4 copy-start.9
  458.5 2.7 copy-start.1
Sparse Core Ops, SparseCore 0:
  30.0 80.6 all-reduce.1
  153.4 60.5 reduce-scatter.1
  216.0 32.1 all-gather.2
  256.6 115.3 all-gather.4
where the time goes:
time: 469 us; the launch traced here: 468 us
  waiting for transfers between devices  284 us (61%)
  matrix products  60.8 us (13%)
  blocking collectives  44.7 us (10%)
  other arithmetic  33.3 us (7%)
  local copies, waits for them, and re-layouts  24.3 us (5%)
  between operations  14.6 us (3%)
  loops' own time  5.3 us (1%)
    all_gather x1, waiting for transfers between devices, body(): full_rows = lax.all_gather(sequence, 'enc', axis=1, tiled=True)  112 us
    psum x1, waiting for transfers between devices, body(): summed = lax.psum(head_terms, 'ctx')  80.8 us
    reduce_scatter x1, waiting for transfers between devices, body(): lax.psum_scatter(jnp.dot(all_hidden, merge_down, preferred_element_type=j...  60.7 us
    all_gather x1, waiting for transfers between devices, body(): vision_all = lax.all_gather(own_vision, 'ctx', axis=0, tiled=True)  31.3 us
    all_gather x1, blocking collectives, body(): all_hidden = lax.all_gather(hidden, 'enc', axis=0, tiled=True)  21.8 us
    dot_general x6, matrix products, update_one_block(): jnp.einsum('gjts,sgd->gjtd', weights.astype(jnp.bfloat16), values_block,...  18.4 us
    all_gather x1, blocking collectives, body(): key_part = lax.all_gather(keys_local, 'ctx', axis=0, tiled=True)  11.5 us
    all_gather x1, blocking collectives, body(): value_part = lax.all_gather(values_local, 'ctx', axis=0, tiled=True)  11.4 us
  transfers between devices with their start and end apart: 4, of which 4 were waited for; matrix products, arithmetic and copies ran while one was open for 1% of the time, Pallas kernels for 0%

commit v1 on v0

--- a/solution.py
+++ b/solution.py
@@ -82,7 +82,9 @@
     attended_patches = image_attention(packed[0], packed[1], packed[2], patch_image)
     flat_heads = attended_patches.transpose(1, 0, 2).reshape(group_rows, head_count * head_width)
     head_terms = jnp.dot(flat_heads, vit_proj, preferred_element_type=jnp.float32)
-    summed = lax.psum(head_terms, "ctx")
+    summed = head_terms
+    for hop in (1, 2, 4):
+        summed = summed + lax.ppermute(summed, "ctx", [(dev, dev ^ hop) for dev in range(8)])
     vit_out = (patches.astype(jnp.float32) + summed).astype(jnp.bfloat16)
     merge_input = layer_norm(lax.optimization_barrier(vit_out), merge_gain)
     unit_inputs = merge_input.reshape(group_rows // 4, 4 * merge_input.shape[1])

time: 469 us -> 567 us (1.21)
  waiting for transfers between devices: 284 us -> 380 us
    ppermute x0 -> x3, waiting for transfers between devices: none -> 176 us  [body(): lax.ppermute(summed, 'ctx', [(dev, dev ^ hop) for dev in range(8)])]
    psum x1 -> x0, waiting for transfers between devices: 80.8 us -> none  [body(): summed = lax.psum(head_terms, 'ctx')]
  transfers between devices with their start and end apart: 4 -> 6, of which waited for: 4 -> 6; matrix products, arithmetic and copies ran while one was open for 1% -> 1% of each run, Pallas kernels for 0% -> 0%
where the time goes in v1:
time: 567 us; the launch traced here: 566 us
  waiting for transfers between devices  380 us (67%)
  matrix products  59.1 us (10%)
  blocking collectives  45.1 us (8%)
  other arithmetic  31.8 us (6%)
  local copies, waits for them, and re-layouts  24.3 us (4%)
  between operations  14.6 us (3%)
  loops' own time  5.88 us (1%)
    ppermute x3, waiting for transfers between devices, body(): lax.ppermute(summed, 'ctx', [(dev, dev ^ hop) for dev in range(8)])  176 us
    all_gather x1, waiting for transfers between devices, body(): full_rows = lax.all_gather(sequence, 'enc', axis=1, tiled=True)  112 us
    reduce_scatter x1, waiting for transfers between devices, body(): lax.psum_scatter(jnp.dot(all_hidden, merge_down, preferred_element_type=j...  60.4 us
    all_gather x1, waiting for transfers between devices, body(): vision_all = lax.all_gather(own_vision, 'ctx', axis=0, tiled=True)  31.5 us
    all_gather x1, blocking collectives, body(): all_hidden = lax.all_gather(hidden, 'enc', axis=0, tiled=True)  22.2 us
    dot_general x6, matrix products, update_one_block(): jnp.einsum('gjts,sgd->gjtd', weights.astype(jnp.bfloat16), values_block,...  18.5 us
    all_gather x1, blocking collectives, body(): value_part = lax.all_gather(values_local, 'ctx', axis=0, tiled=True)  11.6 us
  transfers between devices with their start and end apart: 6, of which 6 were waited for; matrix products, arithmetic and copies ran while one was open for 1% of the time, Pallas kernels for 0%

profile of v1, /device:TPU:0, one launch (start us, length us, event | category | flops | bytes accessed | tf_op | source)
XLA Modules:
  0.0 566.1 jit_solution(14935729042227969305)
XLA Ops:
  11.7 15.2 %while.28 = (s32[]{:T(128)}, bf16[3,2,256,80]{2,3,1,0:T(8,128)(2,1)}, s32[3]{0:T(128)S(1)}, s32[768]{0:T(1024)S(1)}, bf16[2,768,80]{1,2,0:T(8,128)(2,1)S(1)}, /*...) while((s32[]{:T(128)}, ...), condition=%wide.region_5.6_spmd, body=%wide.region_2.5_spmd.sunk | while | flops 128859136 | bytes 6767287 | solution.py:46
  29.1 6.4 %collective-permute-done = f32[768,1280]{1,0:T(8,128)S(1)} collective-permute-done((f32[768,1280]{1,0:T(8,128)S(1)}, f32[768,1280]{1,0:T(8,128)S(1)}, u32[]{:S(2)}, u32[]{:S(2)}) %collective-permute-start) | collective-permute-done | bytes 3932192 | tf_op jit(solution)/shard_map/ppermute | solution.py:87
  38.9 85.3 %collective-permute-done.1 = f32[768,1280]{1,0:T(8,128)S(1)} collective-permute-done((f32[768,1280]{1,0:T(8,128)S(1)}, f32[768,1280]{1,0:T(8,128)S(1)}, u32[]{:S(2)}, u32[]{:S(2)}) %collective-permute-start.1) | collective-permute-done | bytes 3932192 | tf_op jit(solution)/shard_map/ppermute | solution.py:87
  126.5 84.6 %collective-permute-done.2 = f32[768,1280]{1,0:T(8,128)S(1)} collective-permute-done((f32[768,1280]{1,0:T(8,128)S(1)}, f32[768,1280]{1,0:T(8,128)S(1)}, u32[]{:S(2)}, u32[]{:S(2)}) %collective-permute-start.2) | collective-permute-done | bytes 3932192 | tf_op jit(solution)/shard_map/ppermute | solution.py:87
  214.9 4.1 reshape.149
  218.9 6.1 %fusion.61 = bf16[192,640]{1,0:T(8,128)(2,1)S(1)} fusion(bf16[192,5120]{1,0:T(8,128)(2,1)} %reshape.149, bf16[5120,640]{1,0:T(8,128)(2,1)} %param.27), kind=kOutput, calls=%fused_computation.81 | convolution fusion | flops 1266278400 | bytes 8765440 | tf_op jit(solution)/shard_map/dot_general | solution.py:92
  225.1 22.2 %all_gather.15 = bf16[768,640]{1,0:T(8,128)(2,1)S(1)} all-gather(bf16[192,640]{1,0:T(8,128)(2,1)S(1)} %fusion.61), channel_id=1, replica_groups=mesh['enc'=4,'ctx'=8] {'enc'}, dimensions={0}, use_global_device_ids=true | all-gather | bytes 1228800 | tf_op jit(solution)/shard_map/all_gather | solution.py:94
  247.3 4.5 fusion.75
  251.9 60.4 %reduce-scatter.2.cloned.1.call-done = f32[96,2048]{1,0:T(8,128)} async-done(((f32[768,2048]{1,0:T(8,128)}), f32[96,2048]{1,0:T(8,128)}) %reduce-scatter.2.cloned.1.call-update) | async-done | bytes 786448 | tf_op jit(solution)/shard_map/reduce_scatter | solution.py:99
  315.1 31.5 %all-gather.3.cloned.1.call-done = bf16[768,2048]{1,0:T(8,128)(2,1)} async-done(((bf16[96,2048]{1,0:T(8,128)(2,1)}), bf16[768,2048]{1,0:T(8,128)(2,1)}) %all-gather.3.cloned.1.call-update) | async-done | bytes 3145744 | tf_op jit(solution)/shard_map/all_gather | solution.py:105
  346.6 6.7 %gather_fusion = bf16[384,2048]{1,0:T(8,128)(2,1)S(1)} fusion(bf16[768,2048]{1,0:T(8,128)(2,1)} %all-gather.3.cloned.1.call-done, s32[1024]{0:T(1024)S(1)} %pad_clamp_fusion), kind=kCustom, calls=%fused_computation | custom fusion | bytes 3147264 | tf_op jit(solution)/shard_map/jit(_take)/gather | solution.py:106
  358.6 111.6 %all-gather.5.cloned.1.call-done = bf16[384,8192]{1,0:T(8,128)(2,1)} async-done(((bf16[384,2048]{1,0:T(8,128)(2,1)}), bf16[384,8192]{1,0:T(8,128)(2,1)}) %all-gather.5.cloned.1.call-update) | async-done | bytes 6291472 | tf_op jit(solution)/shard_map/all_gather | solution.py:108
  470.2 4.3 fusion.37
  474.8 3.7 convolution_convert_fusion.1
  478.5 11.6 %all_gather.19 = bf16[3072,128]{1,0:T(8,128)(2,1)} all-gather(bf16[384,128]{1,0:T(8,128)(2,1)S(1)} %convolution_convert_fusion.1), channel_id=1, replica_groups=mesh['enc'=4,'ctx'=8] {'ctx'}, dimensions={0}, use_global_device_ids=true | all-gather | bytes 884736 | tf_op jit(solution)/shard_map/all_gather | solution.py:128
  490.2 3.5 convolution_convert_fusion
  494.5 4.6 convolution_convert_fusion.2
  499.2 11.3 %all_gather.18 = bf16[3072,128]{1,0:T(8,128)(2,1)} all-gather(bf16[384,128]{1,0:T(8,128)(2,1)S(1)} %convolution_convert_fusion.2), channel_id=1, replica_groups=mesh['enc'=4,'ctx'=8] {'ctx'}, dimensions={0}, use_global_device_ids=true | all-gather | bytes 884736 | tf_op jit(solution)/shard_map/all_gather | solution.py:127
  510.5 46.4 %conditional.1 = (f32[1,4,384]{2,1,0:T(4,128)}, f32[1,4,384,128]{3,2,1,0:T(8,128)}) conditional(s32[]{:T(128)} %convert_element_type.60, () %tuple.31, (s32[]{:T(128)}, s32[384]{0:T(512)S(1)}, s32[3072]{0:T(1024)}, s32[384]{0:T(512)S(1)}, bf16[3072,128]{1,0:T(8,128)(2,1)}, /*index=5*/bf16[1,4,384,128]{3,2,1,0:T(8,128)(2,1)}, ...), branch_computations={%region_10.11_spmd, %region_11.16_spmd} | conditional | flops 412493696 | bytes 12566875 | solution.py:173
  510.5 46.4 %while.27 = (s32[]{:T(128)}, f32[1,4,384]{2,1,0:T(4,128)S(1)}, f32[1,4,384]{2,1,0:T(4,128)}, f32[1,4,384,128]{3,2,1,0:T(8,128)}, s32[384]{0:T(512)S(1)}, /*index...) while((s32[]{:T(128)}, f32[1,4,384]{2,1,0:T(4,128)S(1)}, ...), condition=%wide.region_15.15_spmd.clone, body=%wide.region_12.14_spmd.clone.sunk | while | flops 412493312 | bytes 12563663 | solution.py:168
  520.2 3.1 fusion.111
  528.0 3.1 fusion.111
  535.9 3.1 fusion.111
  543.8 3.1 fusion.111
  (151 shorter events, 70.7 us)
Async XLA Ops:
  6.5 240.8 %copy-start = (bf16[640,2048]{1,0:T(8,128)(2,1)S(1)}, bf16[640,2048]{1,0:T(8,128)(2,1)}, u32[]{:S(2)}) copy-start(bf16[640,2048]{1,0:T(8,128)(2,1)} %param.28) | copy-start | bytes 7864324
  6.5 3.0 copy-start.13
  6.5 305.7 %reduce-scatter.2.cloned.1.call-start = ((), (), s32[]{:S(2)}) async-start(), calls=%async_computation.1 | async-start | bytes 7077888 | tf_op jit(solution)/shard_map/reduce_scatter | solution.py:99
  6.5 2.3 copy-start.2
  6.6 3.0 copy-start.11
  9.5 2.1 copy-start.8
  11.7 16.1 %copy-start.6 = (bf16[160,1280]{1,0:T(8,128)(2,1)S(1)}, bf16[160,1280]{1,0:T(8,128)(2,1)}, u32[]{:S(2)}) copy-start(bf16[160,1280]{1,0:T(8,128)(2,1)} %param.25) | copy-start | bytes 1228804
  14.1 1.4 copy-start.7
  19.2 1.4 copy-start.7
  24.3 1.4 copy-start.7
  28.6 7.0 %collective-permute-start = (f32[768,1280]{1,0:T(8,128)S(1)}, f32[768,1280]{1,0:T(8,128)S(1)}, u32[]{:S(2)}, u32[]{:S(2)}) collective-permute-start(f32[768,1280]{1,0:T(8,128)S(1)} %fusion.74), channel_id=1, source_target_pairs={{0,1},{1,0},{2,3},{3,2},{4,5},{5,4},{6,7},{7,6},{8,9},{9,8},{10,11... | collective-permute-start | bytes 11796488 | tf_op jit(solution)/shard_map/ppermute | solution.py:87
  36.0 175.2 %copy-start.3 = (bf16[768,1280]{1,0:T(8,128)(2,1)S(1)}, bf16[768,1280]{1,0:T(8,128)(2,1)}, u32[]{:S(2)}) copy-start(bf16[768,1280]{1,0:T(8,128)(2,1)} %param.21) | copy-start | bytes 5898244
  36.0 88.2 %collective-permute-start.1 = (f32[768,1280]{1,0:T(8,128)S(1)}, f32[768,1280]{1,0:T(8,128)S(1)}, u32[]{:S(2)}, u32[]{:S(2)}) collective-permute-start(f32[768,1280]{1,0:T(8,128)S(1)} %add.131), channel_id=1, source_target_pairs={{0,2},{1,3},{2,0},{3,1},{4,6},{5,7},{6,4},{7,5},{8,10},{9,11},{10,... | collective-permute-start | bytes 11796488 | tf_op jit(solution)/shard_map/ppermute | solution.py:87
  124.7 86.5 %collective-permute-start.2 = (f32[768,1280]{1,0:T(8,128)S(1)}, f32[768,1280]{1,0:T(8,128)S(1)}, u32[]{:S(2)}, u32[]{:S(2)}) collective-permute-start(f32[768,1280]{1,0:T(8,128)S(1)} %add.132), channel_id=1, source_target_pairs={{0,4},{1,5},{2,6},{3,7},{4,0},{5,1},{6,2},{7,3},{8,12},{9,13},{10,... | collective-permute-start | bytes 11796488 | tf_op jit(solution)/shard_map/ppermute | solution.py:87
  211.9 1.0 copy-start.9
  251.8 94.7 %all-gather.3.cloned.1.call-start = ((), (), s32[]{:S(2)}) async-start(), calls=%async_computation.2 | async-start | bytes 3538944 | tf_op jit(solution)/shard_map/all_gather | solution.py:105
  314.2 156.0 %all-gather.5.cloned.1.call-start = ((), (), s32[]{:S(2)}) async-start(), calls=%async_computation.3 | async-start | bytes 7864320 | tf_op jit(solution)/shard_map/all_gather | solution.py:108
  315.1 38.2 %copy-start.5 = (bf16[384,2048]{1,0:T(8,128)(2,1)S(1)}, bf16[384,2048]{1,0:T(8,128)(2,1)}, u32[]{:S(2)}) copy-start(bf16[384,2048]{1,0:T(8,128)(2,1)} %param.29) | copy-start | bytes 4718596
  354.7 119.8 %copy-start.12 = (f32[8192]{0:T(1024)S(1)}, f32[8192]{0:T(1024)}, u32[]{:S(2)}) copy-start(f32[8192]{0:T(1024)} %param.32) | copy-start | bytes 98308
  470.2 4.6 copy-start.4
  470.2 19.9 %slice-start = ((s8[8388608]{0:T(1024)(128)(4,1)}), s8[4194304]{0:T(1024)(128)(4,1)S(1)}, s32[]{:S(2)}) async-start(s8[8388608]{0:T(1024)(128)(4,1)} %bitcast.126), calls=%async_computation.4 | async-start | bytes 8388608
  474.8 15.3 %slice-start.1 = ((s8[8388608]{0:T(1024)(128)(4,1)}), s8[4194304]{0:T(1024)(128)(4,1)S(1)}, s32[]{:S(2)}) async-start(s8[8388608]{0:T(1024)(128)(4,1)} %bitcast.126), calls=%async_computation.5 | async-start | bytes 8388608
  490.2 4.4 copy-start.10
  556.8 2.7 copy-start.1
Sparse Core Ops, SparseCore 0:
  252.0 60.2 reduce-scatter.1
  314.3 32.1 all-gather.2
  354.9 115.3 all-gather.4
